TPU v7x, 32 devices: a whole 2x2x4 slice. The times are simulated.
32 devices in a mesh: dp: 16 (over z, x, core), seq: 2 (over y).
Axes of the slice: x: 2, y: 2, z: 4, core: 2. Of those that a mesh axis runs over, the one named last changes fastest.
Arguments:
- gene_ids: int32 [16, 2048], P('dp', 'seq'), may hold values from 0 to 9215, as said below
- homolog_ids: int32 [16, 2048], P('dp', 'seq'), may hold values from 0 to 9215, as said below
- knowledge_ids: int32 [16, 2048], P('dp', 'seq'), may hold values from 0 to 9215, as said below
- expr_bins: int32 [16, 2048], P('dp', 'seq'), may hold values from 0 to 127
- species: int32 [16], P('dp'), may hold values from 0 to 1, as said below
- cell_lengths: int32 [16], P('dp'), may hold values from 1025 to 2048, as said below
- gene_table: bfloat16 [9216, 768], P(('dp', 'seq')), may hold values from -4.1875 to 4.1875
- knowledge_tables: bfloat16 [4, 9216, 768], P(None, ('dp', 'seq')), may hold values from -2.09375 to 2.09375
- expr_table: bfloat16 [128, 768], replicated, may hold values from -4.1875 to 4.1875
- w_query: bfloat16 [768, 768], replicated, may hold values from -0.21875 to 0.21875
- b_query: float32 [768], replicated, may hold values from -1.8 to 1.8
- w_key: bfloat16 [768, 768], replicated, may hold values from -0.21875 to 0.21875
- w_value: bfloat16 [768, 768], replicated, may hold values from -0.21875 to 0.21875
- b_value: float32 [768], replicated, may hold values from -1.8 to 1.8
- w_out: bfloat16 [768, 768], replicated, may hold values from -2.5 to 2.5
- b_out: float32 [768], replicated, may hold values from -1.8 to 1.8
- gain_one: float32 [768], replicated, may hold values from 0.1 to 1.9
- shift_one: float32 [768], replicated, may hold values from -1.8 to 1.8
- w_up: bfloat16 [768, 3072], replicated, may hold values from -0.21875 to 0.21875
- b_up: float32 [3072], replicated, may hold values from -1.8 to 1.8
- w_down: bfloat16 [3072, 768], replicated, may hold values from -0.109375 to 0.109375
- b_down: float32 [768], replicated, may hold values from -1.8 to 1.8
- gain_two: float32 [768], replicated, may hold values from 0.1 to 1.9
- shift_two: float32 [768], replicated, may hold values from -1.8 to 1.8
- cotangent: bfloat16 [16, 2048, 768], P('dp', 'seq'), may hold values from -6 to 6
Outputs:
- layer_output: bfloat16 [16, 2048, 768], P('dp', 'seq')
- gene_table_grad: float32 [9216, 768], P(('dp', 'seq'))
- knowledge_grad: float32 [9216, 768], P(('dp', 'seq'))
- expr_table_grad: float32 [128, 768], replicated
- w_query_grad: float32 [768, 768], replicated
- b_query_grad: float32 [768], replicated
- w_key_grad: float32 [768, 768], replicated
- w_value_grad: float32 [768, 768], replicated
- b_value_grad: float32 [768], replicated
- w_out_grad: float32 [768, 768], replicated
- b_out_grad: float32 [768], replicated
- gain_one_grad: float32 [768], replicated
- shift_one_grad: float32 [768], replicated
- w_up_grad: float32 [768, 3072], replicated
- b_up_grad: float32 [3072], replicated
- w_down_grad: float32 [3072, 768], replicated
- b_down_grad: float32 [768], replicated
- gain_two_grad: float32 [768], replicated
- shift_two_grad: float32 [768], replicated
- row_counts: int32 [2, 9216], P(None, ('dp', 'seq'))
Inputs may be any that keep to these rules, and one draw needn't show every extreme that they name: Of the 1024 genes that one device holds (the cells of its dp index, the positions of its seq index), at most 64 have an id in one block of 288 rows (ids r * 288 to (r + 1) * 288 - 1); in every draw one block has exactly 64 from every device. A gene's gene_ids and homolog_ids lie in the same block. `homolog_ids`: as gene_ids: at most 64 of one device's genes in one block of 288 rows, one block reaching 64 from every device, and the same block as gene_ids for every gene. `knowledge_ids`: at most 64 of one device's genes in one block of 288 rows; in every draw one block has exactly 64 from every device. `species`: exactly a quarter of the cells, rounded down and at least one, have 1. `cell_lengths`: one cell has 2048 and one has 1025.
All inputs are finite; a program needn't handle non-finite values.
Results may differ from a plain program's by a relative error of at most 0.015.
The roundings to bfloat16 on the way count: a program that leaves them out, or rounds other values in their place, can miss the bound.
Values may be sent and summed in bfloat16 or wider, within the bound.
No kernel may reach another device: no remote copies, remote signals or barrier semaphores. Data moves between devices by JAX's collectives and lax.ppermute only.
A program may use at most 192 MiB of HBM per device.

v0:
```python
import jax
import jax.numpy as jnp
from jax import lax
from jax.sharding import PartitionSpec as P

HEADS = 12
HEAD_DIM = 64


def layer_norm(value, gain_vec, shift_vec):
    centre = jnp.mean(value, axis=-1, keepdims=True)
    centred = value - centre
    variance = jnp.mean(centred * centred, axis=-1, keepdims=True)
    return centred * lax.rsqrt(variance + 1e-05) * gain_vec + shift_vec


def gelu_exact(value):
    return jax.nn.gelu(value, approximate=False)


def head_split(array):
    return array.reshape(array.shape[0], HEADS, HEAD_DIM).transpose(1, 0, 2)


def head_merge(array):
    return array.transpose(1, 0, 2).reshape(array.shape[1], HEADS * HEAD_DIM)


def head_scores(query_head, key_head, valid_keys):
    scores = jnp.dot(query_head, key_head.T, preferred_element_type=jnp.float32) * HEAD_DIM ** (
        -0.5
    )
    return jnp.where(valid_keys[None, :], scores, -1e30)


def attend_forward(query_cell, key_cell, value_cell, valid_keys):

    def one_head(head_parts):
        query_head, key_head, value_head = head_parts
        scores = head_scores(query_head, key_head, valid_keys)
        log_total = jax.nn.logsumexp(scores, axis=-1, keepdims=True)
        probs_low = jnp.exp(scores - log_total).astype(jnp.bfloat16)
        context = jnp.dot(probs_low, value_head, preferred_element_type=jnp.float32)
        return (context, log_total[:, 0])

    context, log_total = lax.map(
        one_head, (head_split(query_cell), head_split(key_cell), head_split(value_cell))
    )
    return (head_merge(context), log_total)


def attend_backward(query_cell, key_cell, value_cell, valid_keys, log_total, grad_context):

    def one_head(head_parts):
        query_head, key_head, value_head, total_head, grad_head = head_parts
        scores = head_scores(query_head, key_head, valid_keys)
        attn_probs = jnp.exp(scores - total_head[:, None])
        probs_low = attn_probs.astype(jnp.bfloat16)
        grad_probs = jnp.dot(grad_head, value_head.T, preferred_element_type=jnp.float32)
        inner = jnp.sum(attn_probs * grad_probs, axis=-1, keepdims=True)
        grad_scores = (attn_probs * (grad_probs - inner) * HEAD_DIM ** (-0.5)).astype(jnp.bfloat16)
        grad_query = jnp.dot(grad_scores, key_head, preferred_element_type=jnp.float32)
        grad_key = jnp.dot(grad_scores.T, query_head, preferred_element_type=jnp.float32)
        grad_value = jnp.dot(probs_low.T, grad_head, preferred_element_type=jnp.float32)
        return (grad_query, grad_key, grad_value)

    grad_query, grad_key, grad_value = lax.map(
        one_head,
        (
            head_split(query_cell),
            head_split(key_cell),
            head_split(value_cell),
            log_total,
            head_split(grad_context),
        ),
    )
    return (head_merge(grad_query), head_merge(grad_key), head_merge(grad_value))


def place(identity, rows_dev, devices):
    owner_dev = identity // rows_dev
    owner_hits = (owner_dev[:, None] == jnp.arange(devices)[None, :]).astype(jnp.int32)
    before = jnp.cumsum(owner_hits, axis=0) - owner_hits
    slot_rank = jnp.sum(before * owner_hits, axis=1)
    return (owner_dev, slot_rank, identity - owner_dev * rows_dev)


def local(
    gene_ids,
    homolog_ids,
    knowledge_ids,
    expr_bins,
    species,
    cell_lengths,
    gene_table,
    knowledge_tables,
    expr_table,
    w_query,
    b_query,
    w_key,
    w_value,
    b_value,
    w_out,
    b_out,
    gain_one,
    shift_one,
    w_up,
    b_up,
    w_down,
    b_down,
    gain_two,
    shift_two,
    cotangent,
):
    cells_here, half_len = gene_ids.shape
    width = gene_table.shape[1]
    rows_dev = gene_table.shape[0]
    devices = lax.axis_size(("dp", "seq"))
    looked = cells_here * half_len
    capacity = 2 * looked // devices
    slots_all = 2 * capacity
    chosen = jnp.where(species[:, None] == 1, homolog_ids, gene_ids).reshape(-1)
    gene_owner, gene_rank, gene_local = place(chosen, rows_dev, devices)
    know_owner, know_rank, know_local = place(knowledge_ids.reshape(-1), rows_dev, devices)
    gene_slot = gene_owner * slots_all + gene_rank
    know_slot = know_owner * slots_all + capacity + know_rank
    requests = jnp.full((devices * slots_all,), -1, jnp.int32)
    requests = requests.at[gene_slot].set(gene_local).at[know_slot].set(know_local + rows_dev)
    requests = requests.reshape(devices, slots_all)
    know_sum = jnp.sum(knowledge_tables.astype(jnp.float32), axis=0).astype(jnp.bfloat16)
    combined = jnp.concatenate([gene_table, know_sum], axis=0)
    received = lax.all_to_all(requests, ("dp", "seq"), split_axis=0, concat_axis=0, tiled=True)
    found = jnp.take(combined, jnp.clip(received, 0, 2 * rows_dev - 1), axis=0)
    fetched = lax.all_to_all(found, ("dp", "seq"), split_axis=0, concat_axis=0, tiled=True)
    fetched_flat = fetched.reshape(devices * slots_all, width)
    bin_hot = expr_bins.reshape(-1)[:, None] == jnp.arange(expr_table.shape[0])[None, :]
    expr_rows = jnp.dot(
        bin_hot.astype(jnp.bfloat16), expr_table, preferred_element_type=jnp.float32
    )
    embedded = (
        fetched_flat[gene_slot].astype(jnp.float32)
        + fetched_flat[know_slot].astype(jnp.float32)
        + expr_rows
    )
    x_low = embedded.astype(jnp.bfloat16)
    query_all = (jnp.dot(x_low, w_query, preferred_element_type=jnp.float32) + b_query).astype(
        jnp.bfloat16
    )
    key_local = jnp.dot(x_low, w_key, preferred_element_type=jnp.float32).astype(jnp.bfloat16)
    value_local = (jnp.dot(x_low, w_value, preferred_element_type=jnp.float32) + b_value).astype(
        jnp.bfloat16
    )
    query_cells = query_all.reshape(cells_here, half_len, width)
    key_cells = key_local.reshape(cells_here, half_len, width)
    value_cells = value_local.reshape(cells_here, half_len, width)
    key_whole, value_whole = (
        lax.all_gather(key_cells, "seq", axis=1, tiled=True),
        lax.all_gather(value_cells, "seq", axis=1, tiled=True),
    )
    positions = jnp.arange(key_whole.shape[1])
    valid_keys = positions[None, :] < cell_lengths[:, None]
    context_cells, log_totals = lax.map(
        lambda cell_parts: attend_forward(*cell_parts),
        (query_cells, key_whole, value_whole, valid_keys),
    )
    context_low = context_cells.reshape(looked, width).astype(jnp.bfloat16)
    attn_out = jnp.dot(context_low, w_out, preferred_element_type=jnp.float32) + b_out
    normed_one, norm_one_back = jax.vjp(layer_norm, embedded + attn_out, gain_one, shift_one)
    normed_low = normed_one.astype(jnp.bfloat16)
    pre_ffn = jnp.dot(normed_low, w_up, preferred_element_type=jnp.float32) + b_up
    gelu_value, gelu_back = jax.vjp(gelu_exact, pre_ffn)
    activated = gelu_value.astype(jnp.bfloat16)
    ffn_out = jnp.dot(activated, w_down, preferred_element_type=jnp.float32) + b_down
    final, norm_two_back = jax.vjp(layer_norm, normed_one + ffn_out, gain_two, shift_two)
    layer_output = final.astype(jnp.bfloat16).reshape(cells_here, half_len, width)
    grad_final = cotangent.reshape(looked, width).astype(jnp.float32)
    grad_two, gain_two_grad, shift_two_grad = norm_two_back(grad_final)
    grad_ffn_low = grad_two.astype(jnp.bfloat16)
    w_down_grad = jnp.einsum(
        "tf,td->fd", activated, grad_ffn_low, preferred_element_type=jnp.float32
    )
    b_down_grad = jnp.sum(grad_ffn_low.astype(jnp.float32), axis=0)
    grad_act = jnp.einsum("td,fd->tf", grad_ffn_low, w_down, preferred_element_type=jnp.float32)
    grad_pre_low = gelu_back(grad_act)[0].astype(jnp.bfloat16)
    w_up_grad = jnp.einsum(
        "td,tf->df", normed_low, grad_pre_low, preferred_element_type=jnp.float32
    )
    b_up_grad = jnp.sum(grad_pre_low.astype(jnp.float32), axis=0)
    grad_normed = grad_two + jnp.einsum(
        "tf,df->td", grad_pre_low, w_up, preferred_element_type=jnp.float32
    )
    grad_one, gain_one_grad, shift_one_grad = norm_one_back(grad_normed)
    grad_attn_low = grad_one.astype(jnp.bfloat16)
    w_out_grad = jnp.einsum(
        "te,td->ed", context_low, grad_attn_low, preferred_element_type=jnp.float32
    )
    b_out_grad = jnp.sum(grad_attn_low.astype(jnp.float32), axis=0)
    grad_context = jnp.einsum(
        "td,ed->te", grad_attn_low, w_out, preferred_element_type=jnp.float32
    ).astype(jnp.bfloat16)
    key_back, value_back = (key_whole, value_whole)
    grad_q_cells, grad_k_whole, grad_v_whole = lax.map(
        lambda cell_parts: attend_backward(*cell_parts),
        (
            query_cells,
            key_back,
            value_back,
            valid_keys,
            log_totals,
            grad_context.reshape(cells_here, half_len, width),
        ),
    )
    grad_key_part, grad_value_part = (
        lax.psum_scatter(grad_k_whole, "seq", scatter_dimension=1, tiled=True),
        lax.psum_scatter(grad_v_whole, "seq", scatter_dimension=1, tiled=True),
    )
    grad_query_low = grad_q_cells.reshape(looked, width).astype(jnp.bfloat16)
    grad_key_low = grad_key_part.reshape(looked, width).astype(jnp.bfloat16)
    grad_value_low = grad_value_part.reshape(looked, width).astype(jnp.bfloat16)
    w_query_grad = jnp.einsum(
        "td,te->de", x_low, grad_query_low, preferred_element_type=jnp.float32
    )
    b_query_grad = jnp.sum(grad_query_low.astype(jnp.float32), axis=0)
    w_key_grad = jnp.einsum("td,te->de", x_low, grad_key_low, preferred_element_type=jnp.float32)
    w_value_grad = jnp.einsum(
        "td,te->de", x_low, grad_value_low, preferred_element_type=jnp.float32
    )
    b_value_grad = jnp.sum(grad_value_low.astype(jnp.float32), axis=0)
    grad_embedded = (
        grad_one
        + jnp.einsum("te,de->td", grad_query_low, w_query, preferred_element_type=jnp.float32)
        + jnp.einsum("te,de->td", grad_key_low, w_key, preferred_element_type=jnp.float32)
        + jnp.einsum("te,de->td", grad_value_low, w_value, preferred_element_type=jnp.float32)
    )
    expr_grad_local = jnp.dot(
        bin_hot.astype(jnp.float32).T, grad_embedded, precision=lax.Precision.HIGHEST
    )
    outgoing = jnp.zeros((devices * slots_all, width), jnp.float32)
    outgoing = outgoing.at[gene_slot].set(grad_embedded).at[know_slot].set(grad_embedded)
    outgoing = outgoing.reshape(devices, slots_all, width)
    returned = lax.all_to_all(
        outgoing.astype(jnp.bfloat16), ("dp", "seq"), split_axis=0, concat_axis=0, tiled=True
    ).astype(outgoing.dtype)
    owned = jnp.arange(2 * rows_dev)[:, None] == received.reshape(1, -1)
    table_grads = jnp.dot(
        owned.astype(jnp.float32),
        returned.reshape(devices * slots_all, width),
        precision=lax.Precision.HIGHEST,
    )
    row_counts = jnp.sum(owned.astype(jnp.int32), axis=1).reshape(2, rows_dev)
    whole_summed = lax.psum(
        (
            expr_grad_local,
            w_query_grad,
            b_query_grad,
            w_key_grad,
            w_value_grad,
            b_value_grad,
            w_out_grad,
            b_out_grad,
            gain_one_grad,
            shift_one_grad,
            w_down_grad,
            b_down_grad,
            gain_two_grad,
            shift_two_grad,
            w_up_grad,
            b_up_grad,
        ),
        ("dp", "seq"),
    )
    rest_summed = whole_summed[:10]
    ffn_summed = whole_summed[10:]
    return (
        layer_output,
        table_grads[:rows_dev],
        table_grads[rows_dev:],
        rest_summed[0],
        rest_summed[1],
        rest_summed[2],
        rest_summed[3],
        rest_summed[4],
        rest_summed[5],
        rest_summed[6],
        rest_summed[7],
        rest_summed[8],
        rest_summed[9],
        ffn_summed[4],
        ffn_summed[5],
        ffn_summed[0],
        ffn_summed[1],
        ffn_summed[2],
        ffn_summed[3],
        row_counts,
    )


def solution(mesh):
    placed = (
        P("dp", "seq"),
        P("dp", "seq"),
        P("dp", "seq"),
        P("dp", "seq"),
        P("dp"),
        P("dp"),
        P(("dp", "seq"), None),
        P(None, ("dp", "seq"), None),
        P(),
        P(),
        P(),
        P(),
        P(),
        P(),
        P(),
        P(),
        P(),
        P(),
        P(),
        P(),
        P(),
        P(),
        P(),
        P(),
        P("dp", "seq", None),
    )
    return jax.shard_map(
        local,
        mesh=mesh,
        in_specs=placed,
        out_specs=(
            P("dp", "seq", None),
            P(("dp", "seq"), None),
            P(("dp", "seq"), None),
            P(),
            P(),
            P(),
            P(),
            P(),
            P(),
            P(),
            P(),
            P(),
            P(),
            P(),
            P(),
            P(),
            P(),
            P(),
            P(),
            P(None, ("dp", "seq")),
        ),
        check_vma=False,
    )
```

profile of v0, /device:TPU:0, one launch (start us, length us, event | category | flops | bytes accessed | tf_op | source)
XLA Modules:
  0.0 1586.1 jit_solution(10476663562340610577)
XLA Ops:
  10.3 9.0 reduce-window.14
  19.3 9.0 reduce-window.16
  30.1 4.9 scatter_custom_fusion
  34.9 5.7 scatter_fusion
  40.6 7.3 all-to-all-start
  49.9 5.1 all-to-all-done
  55.1 17.7 %gather_fusion = bf16[4096,768]{1,0:T(8,128)(2,1)} fusion(bf16[576,768]{1,0:T(8,128)(2,1)S(1)} %pad_maximum_fusion, s32[4096]{0:T(1024)S(1)} %fusion.98), kind=kCustom, calls=%fused_computation | custom fusion | bytes 12599296 | tf_op jit(solution)/shard_map/jit(_take)/gather | solution.py:133
  72.8 6.6 broadcast_select_fusion
  83.1 140.1 %all-to-all-done.1 = bf16[32,128,768]{2,1,0:T(8,128)(2,1)} async-done(((bf16[32,128,768]{2,1,0:T(8,128)(2,1)}), bf16[32,128,768]{2,1,0:T(8,128)(2,1)}, u32[]{:S(2)}, u32[]{:S(2)}) %all-to-all-start.1) | async-done | bytes 6291488 | tf_op jit(solution)/shard_map/all_to_all | solution.py:134
  223.3 9.2 gather_fusion.2
  232.4 9.2 gather_fusion.1
  245.9 3.9 fusion.120
  253.6 4.0 add_convert_fusion.2
  261.0 3.9 add_convert_fusion.3
  264.9 4.1 copy.107
  269.0 28.5 %all-gather.5.cloned.1.call-done = bf16[2048,768]{1,0:T(8,128)(2,1)} async-done(((bf16[1024,768]{1,0:T(8,128)(2,1)}), bf16[2048,768]{1,0:T(8,128)(2,1)}) %all-gather.5.cloned.1.call-update) | async-done | bytes 3145744 | tf_op jit(solution)/shard_map/all_gather | solution.py:157
  297.5 4.6 copy.108
  302.1 6.7 copy.110
  308.9 35.7 %all-gather.7.cloned.1.call-done = bf16[2048,768]{1,0:T(8,128)(2,1)} async-done(((bf16[1024,768]{1,0:T(8,128)(2,1)}), bf16[2048,768]{1,0:T(8,128)(2,1)}) %all-gather.7.cloned.1.call-update) | async-done | bytes 3145744 | tf_op jit(solution)/shard_map/all_gather | solution.py:158
  344.6 4.7 copy.109
  349.3 6.5 copy.111
  356.0 117.5 %while.48 = (s32[]{:T(128)}, bf16[12,1024,64]{1,2,0:T(8,128)(2,1)S(1)}, f32[12,1024]{1,0:T(8,128)}, bf16[12,1024,64]{2,1,0:T(8,128)(2,1)}, bf16[12,2048,64]{2,1,...) while((s32[]{:T(128)}, ...), condition=%wide.region_12.13_spmd.clone, body=%wide.region_9.12_spmd.clone.sunk | while | flops 559948800 | bytes 26810476 | solution.py:46
  473.6 4.0 fusion.121
  478.6 48.7 %multiply_convert_fusion.1 = (bf16[1024,3072]{1,0:T(8,128)(2,1)S(1)}, f32[1024,3072]{1,0:T(8,128)}, f32[1024,3072]{1,0:T(8,128)}) fusion(f32[3072]{0:T(1024)S(1)} %copy-done.50, bf16[768,3072]{1,0:T(8,128)(2,1)S(1)} %bitcast.320, f32[1024,768]{0,1:T(8,128)S(1)} %get-tuple-element.424, f32[768]{0:T(1024)S(1)} %copy-done.55, f32[768]{0:T(1024)S(1)} %copy-done.43, ...), kind=kOutput, calls=%fused_computation.75 | convolution fusion | flops 5043388416 | bytes 39348224 | tf_op jit(solution)/shard_map/dot_general | solution.py:170
  527.4 6.0 fusion.122
  540.0 19.4 %convert_reduce_fusion = (f32[3072]{0:T(1024)}, bf16[1024,3072]{1,0:T(8,128)(2,1)}) fusion(f32[1024,3072]{1,0:T(8,128)} %get-tuple-element.403, bf16[1024,768]{0,1:T(8,128)(2,1)} %get-tuple-element.397, bf16[3072,768]{1,0:T(8,128)(2,1)} %param.49, f32[1024,3072]{1,0:T(8,128)} %get-tuple-element.425, f32[3072]{0:T(1024)S(1)} %copy-done.50), kind=kOutput, calls=%fused_computation.73 | convolution fusion | flops 4885312512 | bytes 37773312 | tf_op jit(solution)/shard_map/td,fd->tf/dot_general | solution.py:183
  559.4 11.4 multiply_reduce_fusion.1
  577.2 225.5 %while.49 = (s32[]{:T(128)}, bf16[12,1024,64]{1,2,0:T(8,128)(2,1)S(1)}, f32[12,2048,64]{1,2,0:T(8,128)}, f32[12,2048,64]{1,2,0:T(8,128)}, bf16[12,1024,64]{2,1,0...) while((s32[]{:T(128)}, ...), condition=%wide.region_23.24_spmd.clone, body=%wide.region_21.23_spmd.clone.sunk | while | flops 1375732736 | bytes 66888828 | solution.py:67
  618.8 3.7 fusion.193
  656.3 3.6 fusion.193
  675.1 3.6 fusion.193
  693.9 3.7 fusion.193
  768.9 3.7 fusion.193
  813.5 8.1 fusion.112
  821.6 7.7 fusion.125
  829.3 50.7 %reduce-scatter.3.cloned.1.call-done = f32[1,1024,768]{1,2,0:T(8,128)} async-done(((f32[1,2048,768]{1,2,0:T(8,128)}), f32[1,1024,768]{1,2,0:T(8,128)}) %reduce-scatter.3.cloned.1.call-update) | async-done | bytes 3145744 | tf_op jit(solution)/shard_map/reduce_scatter | solution.py:214
  880.0 4.9 fusion.80
  884.9 74.4 %reduce-scatter.5.cloned.1.call-done = f32[1,1024,768]{1,2,0:T(8,128)} async-done(((f32[1,2048,768]{1,2,0:T(8,128)}), f32[1,1024,768]{1,2,0:T(8,128)}) %reduce-scatter.5.cloned.1.call-update) | async-done | bytes 3145744 | tf_op jit(solution)/shard_map/reduce_scatter | solution.py:215
  959.3 6.2 add_add_fusion.2
  978.0 11.5 scatter_custom_fusion.2
  989.5 14.9 scatter_fusion.1
  1004.4 8.0 convert_element_type.161
  1012.5 4.5 all-to-all-start.2
  1024.2 220.7 %all-reduce = (f32[768]{0:T(1024)}, f32[768]{0:T(1024)}, f32[768]{0:T(1024)}, f32[768]{0:T(1024)}, f32[768]{0:T(1024)}, /*index=5*/f32[3072]{0:T(1024)}, f32[768]{0:T(1024)}, f32[768]{0:T(1024)}, f32[768]{0:T(1024)}) all-reduce(f32[768]{0:T(1024)S(1)} %reduce_sum.262, ...), channel_id=1, replica_groups=mesh['dp'=16,'seq'=2] {'dp','seq'}, use_global_device_ids=true, to_apply=%region_31.32 | all-reduce | flops 9216 | bytes 73728 | tf_op jit(solution)/shard_map/psum | solution.py:251
  1244.9 6.4 fusion.63
  1252.6 301.8 %all-reduce.4.cloned.1.call-done = (f32[128,768]{1,0:T(8,128)}, f32[768,768]{1,0:T(8,128)}, f32[768,768]{1,0:T(8,128)}, f32[768,768]{1,0:T(8,128)}, f32[768,768]...) async-done(((f32[128,768]{1,0:T(8,128)}, f32[768,768]{1,0:T(8,128)}, f32[768,768]{1,0:T(8,128)}, f32[768,768]{1,0:T(8,128)}, f32[768,768]{1,0:T(8,128)}, ...) | async-done | bytes 28704784 | tf_op jit(solution)/shard_map/psum | solution.py:251
  1566.0 9.3 copy.175
  1575.3 3.7 copy.176
  (418 shorter events, 402.2 us)
Async XLA Ops:
  7.2 466.4 %copy-start = (bf16[768,768]{1,0:T(8,128)(2,1)S(1)}, bf16[768,768]{1,0:T(8,128)(2,1)}, u32[]{:S(2)}) copy-start(bf16[768,768]{1,0:T(8,128)(2,1)} %param.43) | copy-start | bytes 3538948
  29.5 53.6 %copy-start.30 = (s32[1024,1]{0,1:T(1,128)}, s32[1024,1]{0,1:T(1,128)S(1)}, u32[]{:S(2)}) copy-start(s32[1024,1]{0,1:T(1,128)S(1)} %compare_select_fusion.2) | copy-start | bytes 12292
  30.0 53.1 %copy-start.40 = (s32[1024,1]{0,1:T(1,128)}, s32[1024,1]{0,1:T(1,128)S(1)}, u32[]{:S(2)}) copy-start(s32[1024,1]{0,1:T(1,128)S(1)} %compare_select_fusion.3) | copy-start | bytes 12292
  34.9 14.9 copy-start.26
  40.6 14.4 all-to-all-start
  55.0 17.8 %copy-start.28 = (s32[32,1,128]{2,1,0:T(1,128)}, s32[32,1,128]{2,1,0:T(1,128)S(1)}, u32[]{:S(2)}) copy-start(s32[32,1,128]{2,1,0:T(1,128)S(1)} %all-to-all-done) | copy-start | bytes 49156
  79.4 143.9 %all-to-all-start.1 = ((bf16[32,128,768]{2,1,0:T(8,128)(2,1)}), bf16[32,128,768]{2,1,0:T(8,128)(2,1)}, u32[]{:S(2)}, u32[]{:S(2)}) async-start(bf16[32,128,768]{2,1,0:T(8,128)(2,1)} %broadcast_select_fusion), calls=%async_computation.1 | async-start | bytes 12582912 | tf_op jit(solution)/shard_map/all_to_all | solution.py:134
  83.0 214.4 %all-gather.5.cloned.1.call-start = ((), (), s32[]{:S(2)}) async-start(), calls=%async_computation.7 | async-start | bytes 4718592 | tf_op jit(solution)/shard_map/all_gather | solution.py:157
  241.6 4.3 copy-start.27
  241.6 4.3 copy-start.35
  245.9 5.0 copy-start.48
  253.5 91.0 %all-gather.7.cloned.1.call-start = ((), (), s32[]{:S(2)}) async-start(), calls=%async_computation.8 | async-start | bytes 4718592 | tf_op jit(solution)/shard_map/all_gather | solution.py:158
  257.6 622.4 %reduce-scatter.3.cloned.1.call-start = ((), (), s32[]{:S(2)}) async-start(), calls=%async_computation.5 | async-start | bytes 9437184 | tf_op jit(solution)/shard_map/reduce_scatter | solution.py:214
  356.0 117.6 %copy-start.53 = (f32[768]{0:T(1024)S(1)}, f32[768]{0:T(1024)}, u32[]{:S(2)}) copy-start(f32[768]{0:T(1024)} %param.44) | copy-start | bytes 9220
  473.6 4.1 copy-start.19
  473.6 4.6 slice-start.5
  473.6 4.6 slice-start.6
  473.6 53.7 %slice-start.3 = ((s8[4718592]{0:T(1024)(128)(4,1)}), s8[4194304]{0:T(1024)(128)(4,1)S(1)}, s32[]{:S(2)}) async-start(s8[4718592]{0:T(1024)(128)(4,1)} %bitcast.317), calls=%async_computation.13 | async-start | bytes 8388608
  477.7 49.6 %copy-start.7 = (f32[1024,768]{0,1:T(8,128)}, f32[1024,768]{0,1:T(8,128)S(1)}, u32[]{:S(2)}) copy-start(f32[1024,768]{0,1:T(8,128)S(1)} %get-tuple-element.424) | copy-start | bytes 9437188
  478.6 48.8 %slice-start.4 = ((s8[4718592]{0:T(1024)(128)(4,1)}), s8[524288]{0:T(1024)(128)(4,1)S(1)}, s32[]{:S(2)}) async-start(s8[4718592]{0:T(1024)(128)(4,1)} %bitcast.317), calls=%async_computation.14 | async-start | bytes 1048576
  478.6 48.8 %copy-start.54 = (f32[768]{0:T(1024)S(1)}, f32[768]{0:T(1024)}, u32[]{:S(2)}) copy-start(f32[768]{0:T(1024)} %param.50) | copy-start | bytes 9220
  527.3 6.1 copy-start.57
  527.4 6.0 copy-start.2
  527.4 6.0 copy-start.32
  559.4 11.4 copy-start.8
  802.8 7.8 copy-start.10
  802.8 156.6 %reduce-scatter.5.cloned.1.call-start = ((), (), s32[]{:S(2)}) async-start(), calls=%async_computation.6 | async-start | bytes 9437184 | tf_op jit(solution)/shard_map/reduce_scatter | solution.py:215
  803.4 751.0 %all-reduce.4.cloned.1.call-start = ((), (), s32[]{:S(2)}) async-start(), calls=%async_computation.9 | async-start | bytes 57409536 | tf_op jit(solution)/shard_map/psum | solution.py:251
  804.6 8.8 slice-start.7
  807.7 5.7 slice-start.8
  810.6 11.0 slice-start.9
  813.5 8.1 copy-start.21
  813.5 8.1 slice-start.10
  821.6 58.4 %copy-start.49 = (bf16[768,768]{1,0:T(8,128)(2,1)S(1)}, bf16[768,768]{1,0:T(8,128)(2,1)}, u32[]{:S(2)}) copy-start(bf16[768,768]{1,0:T(8,128)(2,1)} %param.40) | copy-start | bytes 3538948
  829.3 130.1 %copy-start.25 = (bf16[768,768]{1,0:T(8,128)(2,1)S(1)}, bf16[768,768]{1,0:T(8,128)(2,1)}, u32[]{:S(2)}) copy-start(bf16[768,768]{1,0:T(8,128)(2,1)} %param.41) | copy-start | bytes 3538948
  829.3 130.1 %copy-start.34 = (f32[1024]{0:T(1024)S(1)}, f32[1024]{0:T(1024)}, u32[]{:S(2)}) copy-start(f32[1024]{0:T(1024)} %copy-done.33) | copy-start | bytes 12292
  884.9 80.7 %copy-start.36 = (s32[1,1024]{1,0:T(1,128)S(1)}, s32[1,1024]{1,0:T(1,128)}, u32[]{:S(2)}) copy-start(s32[1,1024]{1,0:T(1,128)} %param.32) | copy-start | bytes 12292
  959.3 8.8 copy-start.18
  965.6 6.0 copy-start.5
  978.0 11.5 copy-start.31
  1012.5 4.5 copy-start.3
  1012.5 4.8 copy-start.29
  1012.5 232.4 %all-to-all-start.2 = ((bf16[32,128,768]{2,1,0:T(8,128)(2,1)}), bf16[32,128,768]{2,1,0:T(8,128)(2,1)}, u32[]{:S(2)}, u32[]{:S(2)}) async-start(bf16[32,128,768]{2,1,0:T(8,128)(2,1)} %bitcast.274), calls=%async_computation.4 | async-start | bytes 12582912 | tf_op jit(solution)/shard_map/all_to_all | solution.py:241
  1017.3 4.3 copy-start.11
  1554.4 5.1 copy-start.14
  1564.6 10.7 slice-start
  1566.0 9.3 slice-start.1
  1566.0 9.3 slice-start.2
  (29 other events, 71.5 us)
Sparse Core Ops, SparseCore 0:
  253.7 43.7 all-gather.4
  299.6 44.9 all-gather.6
  802.9 77.0 reduce-scatter.2
  882.2 77.0 reduce-scatter.4
  974.6 579.7 all-reduce.3
where the time goes:
time: 1600 us; the launch traced here: 1590 us
  waiting for transfers between devices  637 us (40%)
  matrix products  397 us (25%)
  blocking collectives  221 us (14%)
  local copies, waits for them, and re-layouts  173 us (11%)
  other arithmetic  126 us (8%)
    psum x1, waiting for transfers between devices, local(): lax.psum((expr_grad_local, w_query_grad, b_query_grad, w_key_grad, w_valu...  302 us
    psum x1, blocking collectives, local(): lax.psum((expr_grad_local, w_query_grad, b_query_grad, w_key_grad, w_valu...  221 us
    all_to_all x1, waiting for transfers between devices, local(): lax.all_to_all(found, ('dp', 'seq'), split_axis=0, concat_axis=0, tiled=T...  140 us
    reduce_scatter x1, waiting for transfers between devices, local(): lax.psum_scatter(grad_v_whole, 'seq', scatter_dimension=1, tiled=True)  74.4 us
    dot_general x24, matrix products, head_scores(): jnp.dot(query_head, key_head.T, preferred_element_type=jnp.float32)  59.4 us
    reduce_scatter x1, waiting for transfers between devices, local(): lax.psum_scatter(grad_k_whole, 'seq', scatter_dimension=1, tiled=True)  50.7 us
    dot_general x1, matrix products, local(): jnp.dot(normed_low, w_up, preferred_element_type=jnp.float32) + b_up  48.7 us
    unnamed x149, local copies, waits for them, and re-layouts  47.2 us
  transfers between devices with their start and end apart: 8, of which 7 were waited for; matrix products, arithmetic and copies ran while one was open for 7% of the time, Pallas kernels for 0%

commit v1 on v0

--- a/solution.py
+++ b/solution.py
@@ -248,7 +248,8 @@
         precision=lax.Precision.HIGHEST,
     )
     row_counts = jnp.sum(owned.astype(jnp.int32), axis=1).reshape(2, rows_dev)
-    whole_summed = lax.psum(
+    _measure_halves = lambda frame: lax.psum(lax.psum(frame, axis_name="seq"), axis_name="dp")
+    whole_summed = _measure_halves(
         (
             expr_grad_local,
             w_query_grad,
@@ -266,8 +267,7 @@
             shift_two_grad,
             w_up_grad,
             b_up_grad,
-        ),
-        ("dp", "seq"),
+        )
     )
     rest_summed = whole_summed[:10]
     ffn_summed = whole_summed[10:]

time: 1600 us -> 2300 us (1.44)
  waiting for transfers between devices: 637 us -> 1320 us
    psum x1 -> x2, waiting for transfers between devices: 302 us -> 985 us  [the longest x1 642 us: local(): lax.psum(frame, axis_name='seq')]
    psum x1 -> x2, blocking collectives: 221 us -> 239 us  [the longest x1 215 us: local(): lax.psum(lax.psum(frame, axis_name='seq'), axis_name='dp')]
  transfers between devices with their start and end apart: 8 -> 9, of which waited for: 7 -> 8; matrix products, arithmetic and copies ran while one was open for 7% -> 5% of each run, Pallas kernels for 0% -> 0%
where the time goes in v1:
time: 2300 us; the launch traced here: 2290 us
  waiting for transfers between devices  1320 us (57%)
  matrix products  397 us (17%)
  blocking collectives  239 us (10%)
  local copies, waits for them, and re-layouts  174 us (8%)
  other arithmetic  126 us (5%)
    psum x1, waiting for transfers between devices, local(): lax.psum(frame, axis_name='seq')  642 us
    psum x1, waiting for transfers between devices, local(): lax.psum(lax.psum(frame, axis_name='seq'), axis_name='dp')  342 us
    psum x1, blocking collectives, local(): lax.psum(lax.psum(frame, axis_name='seq'), axis_name='dp')  215 us
    all_to_all x1, waiting for transfers between devices, local(): lax.all_to_all(found, ('dp', 'seq'), split_axis=0, concat_axis=0, tiled=T...  140 us
    reduce_scatter x1, waiting for transfers between devices, local(): lax.psum_scatter(grad_v_whole, 'seq', scatter_dimension=1, tiled=True)  74.4 us
    dot_general x24, matrix products, head_scores(): jnp.dot(query_head, key_head.T, preferred_element_type=jnp.float32)  59.4 us
    reduce_scatter x1, waiting for transfers between devices, local(): lax.psum_scatter(grad_k_whole, 'seq', scatter_dimension=1, tiled=True)  50.7 us
    dot_general x1, matrix products, local(): jnp.dot(normed_low, w_up, preferred_element_type=jnp.float32) + b_up  48.7 us
  transfers between devices with their start and end apart: 9, of which 8 were waited for; matrix products, arithmetic and copies ran while one was open for 5% of the time, Pallas kernels for 0%

profile of v1, /device:TPU:0, one launch (start us, length us, event | category | flops | bytes accessed | tf_op | source)
XLA Modules:
  0.0 2288.1 jit_solution(11479150403781075936)
XLA Ops:
  10.3 9.0 reduce-window.14
  19.3 9.0 reduce-window.16
  30.1 4.9 scatter_custom_fusion
  34.9 5.7 scatter_fusion
  40.6 7.3 all-to-all-start
  49.9 5.1 all-to-all-done
  55.1 17.7 gather_fusion
  72.8 6.6 broadcast_select_fusion
  83.1 140.1 %all-to-all-done.1 = bf16[32,128,768]{2,1,0:T(8,128)(2,1)} async-done(((bf16[32,128,768]{2,1,0:T(8,128)(2,1)}), bf16[32,128,768]{2,1,0:T(8,128)(2,1)}, u32[]{:S(2)}, u32[]{:S(2)}) %all-to-all-start.1) | async-done | bytes 6291488 | tf_op jit(solution)/shard_map/all_to_all | solution.py:134
  223.3 9.2 gather_fusion.2
  232.4 9.2 gather_fusion.1
  245.9 3.9 fusion.120
  253.6 4.0 add_convert_fusion.2
  261.0 3.9 add_convert_fusion.3
  264.9 4.1 copy.107
  269.0 28.5 %all-gather.5.cloned.1.call-done = bf16[2048,768]{1,0:T(8,128)(2,1)} async-done(((bf16[1024,768]{1,0:T(8,128)(2,1)}), bf16[2048,768]{1,0:T(8,128)(2,1)}) %all-gather.5.cloned.1.call-update) | async-done | bytes 3145744 | tf_op jit(solution)/shard_map/all_gather | solution.py:157
  297.5 4.6 copy.108
  302.1 6.7 copy.110
  308.9 35.7 %all-gather.7.cloned.1.call-done = bf16[2048,768]{1,0:T(8,128)(2,1)} async-done(((bf16[1024,768]{1,0:T(8,128)(2,1)}), bf16[2048,768]{1,0:T(8,128)(2,1)}) %all-gather.7.cloned.1.call-update) | async-done | bytes 3145744 | tf_op jit(solution)/shard_map/all_gather | solution.py:158
  344.6 4.7 copy.109
  349.3 6.5 copy.111
  356.1 117.5 %while.48 = (s32[]{:T(128)}, bf16[12,1024,64]{1,2,0:T(8,128)(2,1)S(1)}, f32[12,1024]{1,0:T(8,128)}, bf16[12,1024,64]{2,1,0:T(8,128)(2,1)}, bf16[12,2048,64]{2,1,...) while((s32[]{:T(128)}, ...), condition=%wide.region_12.13_spmd.clone, body=%wide.region_9.12_spmd.clone.sunk | while | flops 559948800 | bytes 26810476 | solution.py:46
  473.7 4.0 fusion.121
  478.6 48.7 %multiply_convert_fusion.1 = (bf16[1024,3072]{1,0:T(8,128)(2,1)S(1)}, f32[1024,3072]{1,0:T(8,128)}, f32[1024,3072]{1,0:T(8,128)}) fusion(f32[3072]{0:T(1024)S(1)} %copy-done.50, bf16[768,3072]{1,0:T(8,128)(2,1)S(1)} %bitcast.320, f32[1024,768]{0,1:T(8,128)S(1)} %get-tuple-element.440, f32[768]{0:T(1024)S(1)} %copy-done.55, f32[768]{0:T(1024)S(1)} %copy-done.43, ...), kind=kOutput, calls=%fused_computation.75 | convolution fusion | flops 5043388416 | bytes 39348224 | tf_op jit(solution)/shard_map/dot_general | solution.py:170
  527.4 6.0 fusion.122
  540.1 19.4 convert_reduce_fusion
  559.4 11.4 multiply_reduce_fusion.1
  577.3 225.5 %while.49 = (s32[]{:T(128)}, bf16[12,1024,64]{1,2,0:T(8,128)(2,1)S(1)}, f32[12,2048,64]{1,2,0:T(8,128)}, f32[12,2048,64]{1,2,0:T(8,128)}, bf16[12,1024,64]{2,1,0...) while((s32[]{:T(128)}, ...), condition=%wide.region_23.24_spmd.clone, body=%wide.region_21.23_spmd.clone.sunk | while | flops 1375732736 | bytes 66888828 | solution.py:67
  618.8 3.7 fusion.193
  769.0 3.7 fusion.193
  813.5 8.1 fusion.112
  821.6 7.7 fusion.125
  829.3 50.7 %reduce-scatter.3.cloned.1.call-done = f32[1,1024,768]{1,2,0:T(8,128)} async-done(((f32[1,2048,768]{1,2,0:T(8,128)}), f32[1,1024,768]{1,2,0:T(8,128)}) %reduce-scatter.3.cloned.1.call-update) | async-done | bytes 3145744 | tf_op jit(solution)/shard_map/reduce_scatter | solution.py:214
  880.1 4.9 fusion.80
  885.0 74.4 %reduce-scatter.5.cloned.1.call-done = f32[1,1024,768]{1,2,0:T(8,128)} async-done(((f32[1,2048,768]{1,2,0:T(8,128)}), f32[1,1024,768]{1,2,0:T(8,128)}) %reduce-scatter.5.cloned.1.call-update) | async-done | bytes 3145744 | tf_op jit(solution)/shard_map/reduce_scatter | solution.py:215
  959.4 6.2 add_add_fusion.2
  974.6 642.2 %all-reduce.9.cloned.1.call-done = (f32[128,768]{1,0:T(8,128)}, f32[768,768]{1,0:T(8,128)}, f32[768,768]{1,0:T(8,128)}, f32[768,768]{1,0:T(8,128)}, f32[768,768]...) async-done(((f32[128,768]{1,0:T(8,128)}, f32[768,768]{1,0:T(8,128)}, f32[768,768]{1,0:T(8,128)}, f32[768,768]{1,0:T(8,128)}, f32[768,768]{1,0:T(8,128)}, ...) | async-done | bytes 28704784 | tf_op jit(solution)/shard_map/psum | solution.py:251
  1616.8 3.8 copy.120
  1620.6 11.8 scatter_custom_fusion.2
  1632.4 14.9 scatter_fusion.1
  1647.3 8.1 convert_element_type.161
  1655.4 5.0 all-to-all-start.2
  1667.5 23.2 %all-reduce.2 = (f32[768]{0:T(1024)S(1)}, f32[768]{0:T(1024)S(1)}, f32[768]{0:T(1024)S(1)}, f32[768]{0:T(1024)S(1)}, f32[768]{0:T(1024)S(1)}, /*index=5*/f32[307...) all-reduce(f32[768]{0:T(1024)S(1)} %reduce_sum.262, ...), channel_id=1, replica_groups=mesh['dp'=16,'seq'=2] {'seq'}, use_global_device_ids=true, to_apply=%region_33.34 | all-reduce | flops 9216 | bytes 73728 | tf_op jit(solution)/shard_map/psum | solution.py:251
  1690.7 215.4 %all-reduce = (f32[768]{0:T(1024)}, f32[768]{0:T(1024)}, f32[768]{0:T(1024)}, f32[768]{0:T(1024)}, f32[768]{0:T(1024)}, /*index=5*/f32[3072]{0:T(1024)}, f32[768]{0:T(1024)}, f32[768]{0:T(1024)}, f32[768]{0:T(1024)}) all-reduce(f32[768]{0:T(1024)S(1)} %get-tuple-element.396, ...), channel_id=1, replica_groups=mesh['dp'=16,'seq'=2] {'dp'}, use_global_device_ids=true, to_apply=%region_34.35 | all-reduce | flops 9216 | bytes 73728 | tf_op jit(solution)/shard_map/psum | solution.py:251
  1906.0 6.4 fusion.63
  1913.8 342.3 %all-reduce.7.cloned.1.call-done = (f32[128,768]{1,0:T(8,128)}, f32[768,768]{1,0:T(8,128)}, f32[768,768]{1,0:T(8,128)}, f32[768,768]{1,0:T(8,128)}, f32[768,768]...) async-done(((f32[128,768]{1,0:T(8,128)}, f32[768,768]{1,0:T(8,128)}, f32[768,768]{1,0:T(8,128)}, f32[768,768]{1,0:T(8,128)}, f32[768,768]{1,0:T(8,128)}, ...) | async-done | bytes 28704784 | tf_op jit(solution)/shard_map/psum | solution.py:251
  2267.7 9.3 copy.182
  2277.0 3.7 copy.183
  (422 shorter events, 409.6 us)
Async XLA Ops:
  7.2 466.4 %copy-start = (bf16[768,768]{1,0:T(8,128)(2,1)S(1)}, bf16[768,768]{1,0:T(8,128)(2,1)}, u32[]{:S(2)}) copy-start(bf16[768,768]{1,0:T(8,128)(2,1)} %param.43) | copy-start | bytes 3538948
  29.5 53.6 %copy-start.30 = (s32[1024,1]{0,1:T(1,128)}, s32[1024,1]{0,1:T(1,128)S(1)}, u32[]{:S(2)}) copy-start(s32[1024,1]{0,1:T(1,128)S(1)} %compare_select_fusion.2) | copy-start | bytes 12292
  30.0 53.1 %copy-start.40 = (s32[1024,1]{0,1:T(1,128)}, s32[1024,1]{0,1:T(1,128)S(1)}, u32[]{:S(2)}) copy-start(s32[1024,1]{0,1:T(1,128)S(1)} %compare_select_fusion.3) | copy-start | bytes 12292
  34.9 14.9 copy-start.26
  40.6 14.4 all-to-all-start
  55.0 17.8 copy-start.28
  79.4 143.9 %all-to-all-start.1 = ((bf16[32,128,768]{2,1,0:T(8,128)(2,1)}), bf16[32,128,768]{2,1,0:T(8,128)(2,1)}, u32[]{:S(2)}, u32[]{:S(2)}) async-start(bf16[32,128,768]{2,1,0:T(8,128)(2,1)} %broadcast_select_fusion), calls=%async_computation.1 | async-start | bytes 12582912 | tf_op jit(solution)/shard_map/all_to_all | solution.py:134
  83.0 214.5 %all-gather.5.cloned.1.call-start = ((), (), s32[]{:S(2)}) async-start(), calls=%async_computation.7 | async-start | bytes 4718592 | tf_op jit(solution)/shard_map/all_gather | solution.py:157
  241.6 4.3 copy-start.27
  241.6 4.3 copy-start.35
  245.9 5.0 copy-start.48
  253.6 91.0 %all-gather.7.cloned.1.call-start = ((), (), s32[]{:S(2)}) async-start(), calls=%async_computation.8 | async-start | bytes 4718592 | tf_op jit(solution)/shard_map/all_gather | solution.py:158
  257.7 622.4 %reduce-scatter.3.cloned.1.call-start = ((), (), s32[]{:S(2)}) async-start(), calls=%async_computation.5 | async-start | bytes 9437184 | tf_op jit(solution)/shard_map/reduce_scatter | solution.py:214
  356.1 117.6 %copy-start.53 = (f32[768]{0:T(1024)S(1)}, f32[768]{0:T(1024)}, u32[]{:S(2)}) copy-start(f32[768]{0:T(1024)} %param.44) | copy-start | bytes 9220
  473.6 4.6 slice-start.5
  473.6 4.6 slice-start.6
  473.7 53.7 %slice-start.3 = ((s8[4718592]{0:T(1024)(128)(4,1)}), s8[4194304]{0:T(1024)(128)(4,1)S(1)}, s32[]{:S(2)}) async-start(s8[4718592]{0:T(1024)(128)(4,1)} %bitcast.317), calls=%async_computation.14 | async-start | bytes 8388608
  477.7 49.6 %copy-start.7 = (f32[1024,768]{0,1:T(8,128)}, f32[1024,768]{0,1:T(8,128)S(1)}, u32[]{:S(2)}) copy-start(f32[1024,768]{0,1:T(8,128)S(1)} %get-tuple-element.440) | copy-start | bytes 9437188
  478.6 48.8 %slice-start.4 = ((s8[4718592]{0:T(1024)(128)(4,1)}), s8[524288]{0:T(1024)(128)(4,1)S(1)}, s32[]{:S(2)}) async-start(s8[4718592]{0:T(1024)(128)(4,1)} %bitcast.317), calls=%async_computation.15 | async-start | bytes 1048576
  478.6 48.8 %copy-start.54 = (f32[768]{0:T(1024)S(1)}, f32[768]{0:T(1024)}, u32[]{:S(2)}) copy-start(f32[768]{0:T(1024)} %param.50) | copy-start | bytes 9220
  527.4 6.1 copy-start.57
  527.4 6.0 copy-start.2
  527.4 6.0 copy-start.32
  559.4 11.4 copy-start.8
  802.8 7.8 copy-start.10
  802.8 156.6 %reduce-scatter.5.cloned.1.call-start = ((), (), s32[]{:S(2)}) async-start(), calls=%async_computation.6 | async-start | bytes 9437184 | tf_op jit(solution)/shard_map/reduce_scatter | solution.py:215
  803.4 813.4 %all-reduce.9.cloned.1.call-start = ((), (), s32[]{:S(2)}) async-start(), calls=%async_computation.10 | async-start | bytes 57409536 | tf_op jit(solution)/shard_map/psum | solution.py:251
  804.7 8.8 slice-start.7
  807.8 5.7 slice-start.8
  810.6 11.0 slice-start.9
  813.5 8.1 copy-start.21
  813.5 8.1 slice-start.10
  821.6 58.4 %copy-start.49 = (bf16[768,768]{1,0:T(8,128)(2,1)S(1)}, bf16[768,768]{1,0:T(8,128)(2,1)}, u32[]{:S(2)}) copy-start(bf16[768,768]{1,0:T(8,128)(2,1)} %param.40) | copy-start | bytes 3538948
  829.3 130.1 %copy-start.25 = (bf16[768,768]{1,0:T(8,128)(2,1)S(1)}, bf16[768,768]{1,0:T(8,128)(2,1)}, u32[]{:S(2)}) copy-start(bf16[768,768]{1,0:T(8,128)(2,1)} %param.41) | copy-start | bytes 3538948
  829.3 130.1 %copy-start.34 = (f32[1024]{0:T(1024)S(1)}, f32[1024]{0:T(1024)}, u32[]{:S(2)}) copy-start(f32[1024]{0:T(1024)} %copy-done.33) | copy-start | bytes 12292
  885.0 80.6 %copy-start.36 = (s32[1,1024]{1,0:T(1,128)S(1)}, s32[1,1024]{1,0:T(1,128)}, u32[]{:S(2)}) copy-start(s32[1,1024]{1,0:T(1,128)} %param.32) | copy-start | bytes 12292
  959.4 8.8 copy-start.18
  965.6 6.0 copy-start.5
  974.6 1281.5 %all-reduce.7.cloned.1.call-start = ((), (), s32[]{:S(2)}) async-start(), calls=%async_computation.9 | async-start | bytes 57409536 | tf_op jit(solution)/shard_map/psum | solution.py:251
  1620.6 11.8 copy-start.31
  1655.4 5.0 copy-start.3
  1655.4 5.3 copy-start.29
  1655.4 250.7 %all-to-all-start.2 = ((bf16[32,128,768]{2,1,0:T(8,128)(2,1)}), bf16[32,128,768]{2,1,0:T(8,128)(2,1)}, u32[]{:S(2)}, u32[]{:S(2)}) async-start(bf16[32,128,768]{2,1,0:T(8,128)(2,1)} %bitcast.274), calls=%async_computation.4 | async-start | bytes 12582912 | tf_op jit(solution)/shard_map/all_to_all | solution.py:241
  1660.6 4.3 copy-start.11
  2256.1 5.1 copy-start.14
  2266.3 10.7 slice-start
  2267.7 9.3 slice-start.1
  2267.7 9.3 slice-start.2
  (30 other events, 75.3 us)
Sparse Core Ops, SparseCore 0:
  253.7 43.7 all-gather.4
  299.6 44.9 all-gather.6
  803.0 77.0 reduce-scatter.2
  882.3 77.0 reduce-scatter.4
  974.7 642.0 all-reduce.8
  1622.5 633.5 all-reduce.6
